TPU v7x, 32 devices: a whole 2x2x4 slice. The times are simulated.
32 devices in a mesh: row: 2 (over y), col: 16 (over z, x, core).
Axes of the slice: x: 2, y: 2, z: 4, core: 2. Of those that a mesh axis runs over, the one named last changes fastest.
Arguments:
- blocks: bfloat16 [128, 2048, 128], P('row', 'col'), may hold values from -0.1875 to 0.1875
- block_rows: int32 [2, 1024], P('row', 'col'), may hold values from 0 to 2047, as said below
- block_cols: int32 [2, 1024], P('row', 'col'), may hold values from 0 to 255
- counts: int32 [2, 16], P('row', 'col'), may hold values from 1 to 64, as said below
- start_vectors: float32 [32, 524288], P(None, ('row', 'col')), may hold values from -6 to 6
Outputs:
- vectors: float32 [32, 524288], P(None, ('row', 'col'))
Inputs may be any that keep to these rules, and one draw needn't show every extreme that they name: counts[r, c] is the number of live slots of grid position (r, c); in every draw some position has all 64 slots live. For every grid position (r, c) and every o < 16, exactly 4 of its 64 slots have block_rows[r, c * 64 + s] // 128 == o.
All inputs are finite; a program needn't handle non-finite values.
Results may differ from a plain program's by a relative error of at most 0.0036.
Values may be sent and summed in bfloat16 or wider, within the bound.
A program may use at most 256 MiB of HBM per device.

v0:
```python
import math
import jax
import jax.numpy as jnp
from jax import lax
from jax.sharding import PartitionSpec as P

N = 524288
ITERS = 2


def cholesky_lower(gram_matrix):
    matrix_order = gram_matrix.shape[0]
    positions = jnp.arange(matrix_order)

    def column_step(position, factor):
        before = (positions < position).astype(gram_matrix.dtype)
        target_row = lax.dynamic_index_in_dim(factor, position, 0, keepdims=False) * before
        column = lax.dynamic_index_in_dim(gram_matrix, position, 1, keepdims=False)
        residue = column - jnp.sum(factor * target_row[None, :], axis=1)
        on_diagonal = positions == position
        pivot_value = jnp.sqrt(jnp.sum(jnp.where(on_diagonal, residue, 0.0)))
        values = jnp.where(on_diagonal, pivot_value, residue / pivot_value)
        values = jnp.where(positions >= position, values, 0.0)
        return lax.dynamic_update_index_in_dim(factor, values, position, 1)

    return lax.fori_loop(0, matrix_order, column_step, jnp.zeros_like(gram_matrix))


def lower_inverse(lower_factor):
    matrix_order = lower_factor.shape[0]
    positions = jnp.arange(matrix_order)

    def row_step(position, inverse):
        lower_row = lax.dynamic_index_in_dim(lower_factor, position, 0, keepdims=False)
        before = (positions < position).astype(lower_factor.dtype)
        inner_sum = jnp.sum((lower_row * before)[:, None] * inverse, axis=0)
        unit_row = (positions == position).astype(lower_factor.dtype)
        pivot_value = jnp.sum(lower_row * unit_row)
        return lax.dynamic_update_index_in_dim(
            inverse, (unit_row - inner_sum) / pivot_value, position, 0
        )

    return lax.fori_loop(0, matrix_order, row_step, jnp.zeros_like(lower_factor))


def accumulate(blocks, rows_index, cols_index, live_count, row_panel, col_panel):
    slot_count, block_size = (blocks.shape[0], blocks.shape[1])
    vector_count = row_panel.shape[0]
    row_blocks = row_panel.reshape(vector_count, -1, block_size)
    col_blocks = col_panel.reshape(vector_count, -1, block_size)
    group_size = math.gcd(slot_count, 64)
    turn_count = (live_count + group_size - 1) // group_size
    slot_offsets = jnp.arange(group_size, dtype=jnp.int32)

    def one_group(turn_index, partial_sums):
        row_sums, col_sums = partial_sums
        first_slot = turn_index * group_size
        live_mask = (first_slot + slot_offsets < live_count).astype(jnp.float32)
        from_cols = jnp.take(col_blocks, cols_index, axis=1)
        from_rows = jnp.take(row_blocks, rows_index, axis=1)
        to_cols = jnp.einsum("kgi,gij->kgj", from_rows, blocks, preferred_element_type=jnp.float32)
        col_sums = col_sums.at[:, cols_index].add(to_cols * live_mask[None, :, None])
        to_rows = jnp.einsum("kgj,gij->kgi", from_cols, blocks, preferred_element_type=jnp.float32)
        row_sums = row_sums.at[:, rows_index].add(to_rows * live_mask[None, :, None])
        return (row_sums, col_sums)

    row_start = jnp.zeros(row_blocks.shape, jnp.float32)
    initial = (row_start, jnp.zeros(col_blocks.shape, jnp.float32))
    return lax.fori_loop(0, turn_count, one_group, initial)


def per_device(blocks, block_rows, block_cols, counts, start_vectors):
    live_count = counts[0, 0]
    rows_index = block_rows[0]
    cols_index = block_cols[0]
    vectors = start_vectors
    for iteration in range(ITERS):
        rounded = vectors.astype(jnp.bfloat16)
        vector_count = rounded.shape[0]
        col_panel = lax.all_gather(rounded, "row", axis=1, tiled=True)
        row_panel = lax.all_gather(rounded, "col", axis=1, tiled=True)
        row_sums, col_sums = accumulate(
            blocks, rows_index, cols_index, live_count, row_panel, col_panel
        )
        from_row_group = lax.psum_scatter(
            row_sums.reshape(vector_count, -1), "col", scatter_dimension=1, tiled=True
        )
        from_col_group = lax.psum_scatter(
            col_sums.reshape(vector_count, -1), "row", scatter_dimension=1, tiled=True
        )
        product = from_row_group + from_col_group
        local_gram = jnp.dot(
            product, product.T, precision=lax.Precision.HIGHEST, preferred_element_type=jnp.float32
        )
        gram_matrix = lax.psum(local_gram, ("row", "col")) / N
        inverse = lower_inverse(cholesky_lower(gram_matrix))
        vectors = jnp.dot(
            inverse, product, precision=lax.Precision.HIGHEST, preferred_element_type=jnp.float32
        )
    return vectors


def solution(mesh):
    placed = (
        P("row", "col", None),
        P("row", "col"),
        P("row", "col"),
        P("row", "col"),
        P(None, ("row", "col")),
    )
    return jax.shard_map(
        per_device, mesh=mesh, in_specs=placed, out_specs=P(None, ("row", "col")), check_vma=False
    )
```

profile of v0, /device:TPU:0, one launch (start us, length us, event | category | flops | bytes accessed | tf_op | source)
XLA Modules:
  0.0 1549.7 jit_solution(5209276909103308987)
XLA Ops:
  6.5 2.8 convert_element_type.66
  9.4 0.7 all-gather.7.cloned.1.call-update
  11.0 34.4 %all-gather.5.cloned.1.call-done = bf16[32,32768]{1,0:T(8,128)(2,1)} async-done(((bf16[32,16384]{1,0:T(8,128)(2,1)}), bf16[32,32768]{1,0:T(8,128)(2,1)}) %all-gather.5.cloned.1.call-update) | async-done | bytes 2097168 | tf_op jit(solution)/shard_map/all_gather | solution.py:80
  45.4 3.3 copy_bitcast_fusion.7
  48.6 2.2 gather_fusion
  50.9 2.2 fusion.34
  53.1 121.4 %all-gather.7.cloned.1.call-done = bf16[32,262144]{1,0:T(8,128)(2,1)} async-done(((bf16[32,16384]{1,0:T(8,128)(2,1)}), bf16[32,262144]{1,0:T(8,128)(2,1)}) %all-gather.7.cloned.1.call-update) | async-done | bytes 16777232 | tf_op jit(solution)/shard_map/all_gather | solution.py:81
  174.5 14.5 copy_bitcast_fusion.3
  189.0 6.4 gather_fusion.1
  195.4 1.7 fusion.32
  197.1 11.3 broadcast.314.clone
  208.4 2.6 broadcast.315.clone
  210.9 20.4 %while.90 = (s32[]{:T(128)}, f32[32,2048,128]{2,0,1:T(8,128)}, f32[32,256,128]{2,0,1:T(8,128)}, s32[]{:T(128)}, s32[64]{0:T(128)S(1)}, /*index=5*/s32[]{:T(128)}...) while((s32[]{:T(128)}, f32[32,2048,128]{2,0,1:T(8,128)}, ...), condition=%wide.region_3.6_spmd.clone, body=%wide.region_0.5_spmd.clone.sunk | while | flops 1049155 | bytes 10487937 | solution.py:69
  211.6 2.7 broadcast_multiply_fusion.8
  214.3 9.0 scatter_fusion
  223.3 8.0 scatter_fusion.1
  231.3 4.4 copy_bitcast_fusion.5
  235.8 22.6 %copy_bitcast_fusion.1 = f32[32,262144]{1,0:T(8,128)} fusion(f32[32,2048,128]{2,0,1:T(8,128)} %get-tuple-element.609), kind=kLoop, calls=%fused_computation.69 | loop fusion | bytes 67108864 | tf_op jit(solution)/shard_map/reshape | solution.py:86
  258.5 30.0 %reduce-scatter.7.cloned.1.call-done = f32[32,16384]{1,0:T(8,128)} async-done(((f32[32,32768]{1,0:T(8,128)}), f32[32,16384]{1,0:T(8,128)}) %reduce-scatter.7.cloned.1.call-update) | async-done | bytes 2097168 | tf_op jit(solution)/shard_map/reduce_scatter | solution.py:88
  288.4 337.4 %reduce-scatter.5.cloned.1.call-done = f32[32,16384]{1,0:T(8,128)} async-done(((f32[32,262144]{1,0:T(8,128)}), f32[32,16384]{1,0:T(8,128)}) %reduce-scatter.5.cloned.1.call-update) | async-done | bytes 2097168 | tf_op jit(solution)/shard_map/reduce_scatter | solution.py:85
  625.8 2.4 add.220
  628.2 1.3 copy-done.2
  629.5 1.8 fusion.52
  631.3 39.1 %psum.14 = f32[32,32]{1,0:T(8,128)S(1)} all-reduce(f32[32,32]{1,0:T(8,128)S(1)} %fusion.52), channel_id=1, replica_groups=mesh['row'=2,'col'=16] {'row','col'}, use_global_device_ids=true, to_apply=%region_6.9 | all-reduce | flops 1024 | bytes 8192 | tf_op jit(solution)/shard_map/psum | solution.py:95
  670.4 58.1 %while.92 = (s32[]{:T(128)}, f32[32,32]{1,0:T(8,128)S(1)}, f32[32,32]{0,1:T(8,128)S(1)}, s32[]{:T(128)}, s32[]{:T(128)}) while((s32[]{:T(128)}, f32[32,32]{1,0:T(8,128)S(1)}, f32[32,32]{0,1:T(8,128)S(1)}, s32[]{:T(128)}, s32[]{:T(128)}) %tuple.192), condition=%wide.region_10.13_spmd.clone.clone, body=%wide.region_7.12_spmd.clone.clone.sunk | while | flops 2401 | bytes 8913 | solution.py:26
  670.6 0.7 fusion.88
  672.3 0.7 fusion.88
  674.1 0.7 fusion.88
  676.0 0.7 fusion.88
  677.8 0.7 fusion.88
  679.6 0.7 fusion.88
  685.1 0.7 fusion.88
  690.5 0.7 fusion.88
  708.7 0.7 fusion.88
  714.2 0.7 fusion.88
  719.6 0.7 fusion.88
  725.1 0.7 fusion.88
  728.6 49.0 %while.93 = (s32[]{:T(128)}, f32[32,32]{1,0:T(8,128)S(1)}, f32[32,32]{1,0:T(8,128)S(1)}, s32[]{:T(128)}, s32[]{:T(128)}) while((s32[]{:T(128)}, f32[32,32]{1,0:T(8,128)S(1)}, f32[32,32]{1,0:T(8,128)S(1)}, s32[]{:T(128)}, s32[]{:T(128)}) %tuple.195), condition=%wide.region_14.17_spmd.clone.clone, body=%wide.region_11.16_spmd.clone.clone.sunk | while | flops 2305 | bytes 6221 | solution.py:43
  777.6 4.4 convolution_convert_fusion
  782.8 32.2 %all-gather.9.cloned.1.call-done = bf16[32,32768]{1,0:T(8,128)(2,1)} async-done(((bf16[32,16384]{1,0:T(8,128)(2,1)}), bf16[32,32768]{1,0:T(8,128)(2,1)}) %all-gather.9.cloned.1.call-update) | async-done | bytes 2097168 | tf_op jit(solution)/shard_map/all_gather | solution.py:80
  815.1 3.3 copy_bitcast_fusion.6
  818.3 2.2 gather_fusion.2
  820.6 2.2 fusion.30
  822.8 121.5 %all-gather.11.cloned.1.call-done = bf16[32,262144]{1,0:T(8,128)(2,1)} async-done(((bf16[32,16384]{1,0:T(8,128)(2,1)}), bf16[32,262144]{1,0:T(8,128)(2,1)}) %all-gather.11.cloned.1.call-update) | async-done | bytes 16777232 | tf_op jit(solution)/shard_map/all_gather | solution.py:81
  944.3 14.5 copy_bitcast_fusion.2
  958.8 6.4 gather_fusion.3
  965.2 1.7 fusion.28
  966.9 11.3 broadcast.314
  978.2 2.6 broadcast.315
  980.7 20.4 %while.91 = (s32[]{:T(128)}, f32[32,2048,128]{2,0,1:T(8,128)}, f32[32,256,128]{2,0,1:T(8,128)}, s32[]{:T(128)}, s32[64]{0:T(128)S(1)}, /*index=5*/s32[]{:T(128)}...) while((s32[]{:T(128)}, f32[32,2048,128]{2,0,1:T(8,128)}, ...), condition=%wide.region_18.21_spmd.clone, body=%wide.region_15.20_spmd.clone.sunk | while | flops 1049155 | bytes 10487937 | solution.py:69
  981.4 2.7 broadcast_multiply_fusion.9
  984.1 9.0 scatter_fusion.2
  993.1 8.0 scatter_fusion.3
  1001.1 4.4 copy_bitcast_fusion.4
  1005.6 22.6 %copy_bitcast_fusion = f32[32,262144]{1,0:T(8,128)} fusion(f32[32,2048,128]{2,0,1:T(8,128)} %get-tuple-element.613), kind=kLoop, calls=%fused_computation.68 | loop fusion | bytes 67108864 | tf_op jit(solution)/shard_map/reshape | solution.py:86
  1028.2 30.0 %reduce-scatter.11.cloned.1.call-done = f32[32,16384]{1,0:T(8,128)} async-done(((f32[32,32768]{1,0:T(8,128)}), f32[32,16384]{1,0:T(8,128)}) %reduce-scatter.11.cloned.1.call-update) | async-done | bytes 2097168 | tf_op jit(solution)/shard_map/reduce_scatter | solution.py:88
  1058.2 336.9 %reduce-scatter.9.cloned.1.call-done = f32[32,16384]{1,0:T(8,128)} async-done(((f32[32,262144]{1,0:T(8,128)}), f32[32,16384]{1,0:T(8,128)}) %reduce-scatter.9.cloned.1.call-update) | async-done | bytes 2097168 | tf_op jit(solution)/shard_map/reduce_scatter | solution.py:85
  1395.2 2.4 add.221
  1397.6 1.3 copy-done.1
  1398.9 1.8 fusion.53
  1400.7 39.0 %psum.15 = f32[32,32]{1,0:T(8,128)S(1)} all-reduce(f32[32,32]{1,0:T(8,128)S(1)} %fusion.53), channel_id=1, replica_groups=mesh['row'=2,'col'=16] {'row','col'}, use_global_device_ids=true, to_apply=%region_21.24 | all-reduce | flops 1024 | bytes 8192 | tf_op jit(solution)/shard_map/psum | solution.py:95
  1439.8 53.9 %while.94 = (s32[]{:T(128)}, f32[32,32]{1,0:T(8,128)S(1)}, f32[32,32]{0,1:T(8,128)S(1)}, s32[]{:T(128)}, s32[]{:T(128)}) while((s32[]{:T(128)}, f32[32,32]{1,0:T(8,128)S(1)}, f32[32,32]{0,1:T(8,128)S(1)}, s32[]{:T(128)}, s32[]{:T(128)}) %tuple.201), condition=%wide.region_25.28_spmd.clone.clone, body=%wide.region_22.27_spmd.clone.clone.sunk | while | flops 2401 | bytes 8913 | solution.py:26
  1493.7 44.3 %while.95 = (s32[]{:T(128)}, f32[32,32]{1,0:T(8,128)S(1)}, f32[32,32]{1,0:T(8,128)S(1)}, s32[]{:T(128)}, s32[]{:T(128)}) while((s32[]{:T(128)}, f32[32,32]{1,0:T(8,128)S(1)}, f32[32,32]{1,0:T(8,128)S(1)}, s32[]{:T(128)}, s32[]{:T(128)}) %tuple.204), condition=%wide.region_29.32_spmd.clone.clone, body=%wide.region_26.31_spmd.clone.clone.sunk | while | flops 2305 | bytes 6221 | solution.py:43
  1538.1 4.8 fusion.54
  (669 shorter events, 151.3 us)
Async XLA Ops:
  6.5 44.4 %copy-start = (bf16[64,128,128]{2,1,0:T(8,128)(2,1)S(1)}, bf16[64,128,128]{2,1,0:T(8,128)(2,1)}, u32[]{:S(2)}) copy-start(bf16[64,128,128]{2,1,0:T(8,128)(2,1)} %param.21) | copy-start | bytes 6291460
  6.5 4.3 copy-start.3
  6.5 4.4 copy-start.4
  6.5 38.8 %all-gather.5.cloned.1.call-start = ((), (), s32[]{:S(2)}) async-start(), calls=%async_computation.4 | async-start | bytes 3145728 | tf_op jit(solution)/shard_map/all_gather | solution.py:80
  9.4 165.1 %all-gather.7.cloned.1.call-start = ((), (), s32[]{:S(2)}) async-start(), calls=%async_computation.5 | async-start | bytes 17825792 | tf_op jit(solution)/shard_map/all_gather | solution.py:81
  10.2 278.3 %reduce-scatter.7.cloned.1.call-start = ((), (), s32[]{:S(2)}) async-start(), calls=%async_computation.7 | async-start | bytes 6291456 | tf_op jit(solution)/shard_map/reduce_scatter | solution.py:88
  235.8 390.0 %reduce-scatter.5.cloned.1.call-start = ((), (), s32[]{:S(2)}) async-start(), calls=%async_computation.6 | async-start | bytes 35651584 | tf_op jit(solution)/shard_map/reduce_scatter | solution.py:85
  258.4 556.7 %all-gather.9.cloned.1.call-start = ((), (), s32[]{:S(2)}) async-start(), calls=%async_computation.8 | async-start | bytes 3145728 | tf_op jit(solution)/shard_map/all_gather | solution.py:80
  628.2 1.3 copy-start.2
  782.0 162.3 %all-gather.11.cloned.1.call-start = ((), (), s32[]{:S(2)}) async-start(), calls=%async_computation.9 | async-start | bytes 17825792 | tf_op jit(solution)/shard_map/all_gather | solution.py:81
  782.6 275.6 %reduce-scatter.11.cloned.1.call-start = ((), (), s32[]{:S(2)}) async-start(), calls=%async_computation.11 | async-start | bytes 6291456 | tf_op jit(solution)/shard_map/reduce_scatter | solution.py:88
  1005.6 389.6 %reduce-scatter.9.cloned.1.call-start = ((), (), s32[]{:S(2)}) async-start(), calls=%async_computation.10 | async-start | bytes 35651584 | tf_op jit(solution)/shard_map/reduce_scatter | solution.py:85
  1397.6 1.4 copy-start.1
Sparse Core Ops, SparseCore 0:
  9.5 35.8 all-gather.4
  47.6 126.9 all-gather.6
  235.9 52.4 reduce-scatter.6
  293.1 332.6 reduce-scatter.4
  782.1 32.8 all-gather.8
  817.4 126.9 all-gather.10
  1005.7 52.4 reduce-scatter.10
  1062.5 332.6 reduce-scatter.8
where the time goes:
time: 1550 us
  waiting for transfers between devices  1050 us (68%)
  other arithmetic  189 us (12%)
  local copies, waits for them, and re-layouts  153 us (10%)
  blocking collectives  78.1 us (5%)
  loops' own time  48.3 us (3%)
  matrix products  20.5 us (1%)
    reduce_scatter x2, waiting for transfers between devices, per_device(): lax.psum_scatter(row_sums.reshape(vector_count, -1), 'col', scatter_dimen...  674 us
    all_gather x2, waiting for transfers between devices, per_device(): row_panel = lax.all_gather(rounded, 'col', axis=1, tiled=True)  243 us
    psum x2, blocking collectives, per_device(): gram_matrix = lax.psum(local_gram, ('row', 'col')) / N  78.1 us
    all_gather x2, waiting for transfers between devices, per_device(): col_panel = lax.all_gather(rounded, 'row', axis=1, tiled=True)  66.7 us
    reduce_scatter x2, waiting for transfers between devices, per_device(): lax.psum_scatter(col_sums.reshape(vector_count, -1), 'row', scatter_dimen...  60 us
    another operation x2, loops' own time, cholesky_lower(): lax.fori_loop(0, matrix_order, column_step, jnp.zeros_like(gram_matrix))  46.9 us
    reshape x2, local copies, waits for them, and re-layouts, per_device(): row_sums.reshape(vector_count, -1)  45.2 us
    reduce_sum x64, other arithmetic, column_step(): pivot_value = jnp.sqrt(jnp.sum(jnp.where(on_diagonal, residue, 0.0)))  42.8 us
  transfers between devices with their start and end apart: 8, of which 8 were waited for; matrix products, arithmetic and copies ran while one was open for 4% of the time, Pallas kernels for 0%

commit v1 on v0

--- a/solution.py
+++ b/solution.py
@@ -6,6 +6,22 @@
 
 N = 524288
 ITERS = 2
+
+
+def ring_gather(x, axis, dim):
+    ways, here, step = (lax.axis_size(axis), lax.axis_index(axis), x.shape[dim])
+    lengths = [n * ways if d == dim else n for d, n in enumerate(x.shape)]
+    full = lax.dynamic_update_slice_in_dim(jnp.zeros(lengths, x.dtype), x, here * step, axis=dim)
+    going_up = going_down = x
+    for far in range(1, ways // 2 + 1):
+        going_up = lax.ppermute(going_up, axis, [(d, (d + 1) % ways) for d in range(ways)])
+        full = lax.dynamic_update_slice_in_dim(full, going_up, (here - far) % ways * step, axis=dim)
+        if 2 * far < ways:
+            going_down = lax.ppermute(going_down, axis, [(d, (d - 1) % ways) for d in range(ways)])
+            full = lax.dynamic_update_slice_in_dim(
+                full, going_down, (here + far) % ways * step, axis=dim
+            )
+    return full
 
 
 def cholesky_lower(gram_matrix):
@@ -78,7 +94,7 @@
         rounded = vectors.astype(jnp.bfloat16)
         vector_count = rounded.shape[0]
         col_panel = lax.all_gather(rounded, "row", axis=1, tiled=True)
-        row_panel = lax.all_gather(rounded, "col", axis=1, tiled=True)
+        row_panel = ring_gather(rounded, "col", 1)
         row_sums, col_sums = accumulate(
             blocks, rows_index, cols_index, live_count, row_panel, col_panel
         )

time: 1550 us -> 1630 us (1.052)
  starting transfers between devices: 0.47 us -> 233 us
  waiting for transfers between devices: 1050 us -> 829 us
  local copies, waits for them, and re-layouts: 153 us -> 212 us
    all_gather x2 -> x0, waiting for transfers between devices: 243 us -> none  [per_device(): row_panel = lax.all_gather(rounded, 'col', axis=1, tiled=True)]
    ppermute x0 -> x30, starting transfers between devices: none -> 233 us  [the longest x16 222 us: ring_gather(): lax.ppermute(going_up, axis, [(d, (d + 1) % ways) for d in range(ways)])]
    ppermute x0 -> x30, waiting for transfers between devices: none -> 72.2 us  [the longest x16 72.2 us: ring_gather(): lax.ppermute(going_up, axis, [(d, (d + 1) % ways) for d in range(ways)])]
    all_gather x2, waiting for transfers between devices: 66.7 us -> 0.01 us  [per_device(): col_panel = lax.all_gather(rounded, 'row', axis=1, tiled=True)]
    dynamic_update_slice x0 -> x30, local copies, waits for them, and re-layouts: none -> 45.4 us  [the longest x16 23.7 us: ring_gather(): lax.dynamic_update_slice_in_dim(full, going_up, (here - far) % ways * ste...]
    reduce_scatter x2, waiting for transfers between devices: 60 us -> 82.6 us  [per_device(): lax.psum_scatter(col_sums.reshape(vector_count, -1), 'row', scatter_dimen...]
    another operation x8 -> x10, local copies, waits for them, and re-layouts: 27.7 us -> 40.4 us
  transfers between devices with their start and end apart: 8 -> 36, of which waited for: 8 -> 18; matrix products, arithmetic and copies ran while one was open for 4% -> 6% of each run, Pallas kernels for 0% -> 0%
where the time goes in v1:
time: 1630 us; the launch traced here: 1620 us
  waiting for transfers between devices  829 us (51%)
  starting transfers between devices  233 us (14%)
  local copies, waits for them, and re-layouts  212 us (13%)
  other arithmetic  187 us (11%)
  blocking collectives  78.3 us (5%)
  loops' own time  50.4 us (3%)
  matrix products  19 us (1%)
    reduce_scatter x2, waiting for transfers between devices, per_device(): lax.psum_scatter(row_sums.reshape(vector_count, -1), 'col', scatter_dimen...  674 us
    ppermute x16, starting transfers between devices, ring_gather(): lax.ppermute(going_up, axis, [(d, (d + 1) % ways) for d in range(ways)])  222 us
    reduce_scatter x2, waiting for transfers between devices, per_device(): lax.psum_scatter(col_sums.reshape(vector_count, -1), 'row', scatter_dimen...  82.6 us
    psum x2, blocking collectives, per_device(): gram_matrix = lax.psum(local_gram, ('row', 'col')) / N  78.3 us
    ppermute x16, waiting for transfers between devices, ring_gather(): lax.ppermute(going_up, axis, [(d, (d + 1) % ways) for d in range(ways)])  72.2 us
    another operation x2, loops' own time, cholesky_lower(): lax.fori_loop(0, matrix_order, column_step, jnp.zeros_like(gram_matrix))  48.9 us
    reshape x2, local copies, waits for them, and re-layouts, per_device(): row_sums.reshape(vector_count, -1)  45.6 us
    reduce_sum x64, other arithmetic, column_step(): pivot_value = jnp.sqrt(jnp.sum(jnp.where(on_diagonal, residue, 0.0)))  44 us
  transfers between devices with their start and end apart: 36, of which 18 were waited for; matrix products, arithmetic and copies ran while one was open for 6% of the time, Pallas kernels for 0%

profile of v1, /device:TPU:0, one launch (start us, length us, event | category | flops | bytes accessed | tf_op | source)
XLA Modules:
  0.0 1623.6 jit_solution(10120990595641245166)
XLA Ops:
  6.6 6.7 broadcast.334.clone
  14.8 5.0 collective-permute-start.1
  20.9 11.6 collective-permute-done
  32.5 7.9 collective-permute-start.2
  44.9 4.9 collective-permute-done.2
  49.8 15.6 collective-permute-start.4
  69.9 3.3 copy_bitcast_fusion.7
  77.6 14.6 collective-permute-start.6
  98.7 8.3 collective-permute-done.6
  107.0 10.0 collective-permute-start.8
  119.0 5.8 collective-permute-done.8
  124.8 16.2 collective-permute-start.10
  143.0 5.1 collective-permute-done.10
  148.1 17.6 %collective-permute-start.12 = (bf16[32,16384]{1,0:T(8,128)(2,1)S(1)}, bf16[32,16384]{1,0:T(8,128)(2,1)S(1)}, u32[]{:S(2)}, u32[]{:S(2)}) collective-permute-start(bf16[32,16384]{1,0:T(8,128)(2,1)S(1)} %collective-permute-done.10), channel_id=1, source_target_pairs={{0,1},{1,2},{2,3},{3,4},{4,5},{5,6},{6,7},{7,8},{8,9},{9,10},{10,1... | collective-permute-start | bytes 3145736 | tf_op jit(solution)/shard_map/ppermute | solution.py:17
  167.7 5.7 collective-permute-done.12
  173.5 16.9 %collective-permute-start.14 = (bf16[32,16384]{1,0:T(8,128)(2,1)S(1)}, bf16[32,16384]{1,0:T(8,128)(2,1)S(1)}, u32[]{:S(2)}, u32[]{:S(2)}) collective-permute-start(bf16[32,16384]{1,0:T(8,128)(2,1)S(1)} %collective-permute-done.12), channel_id=1, source_target_pairs={{0,1},{1,2},{2,3},{3,4},{4,5},{5,6},{6,7},{7,8},{8,9},{9,10},{10,1... | collective-permute-start | bytes 3145736 | tf_op jit(solution)/shard_map/ppermute | solution.py:17
  192.5 6.3 collective-permute-done.14
  199.8 14.5 copy_bitcast_fusion.3
  214.3 6.4 gather_fusion.1
  222.4 11.3 broadcast.332.clone
  233.7 2.6 broadcast.333.clone
  236.3 20.4 %while.90 = (s32[]{:T(128)}, f32[32,2048,128]{2,0,1:T(8,128)}, f32[32,256,128]{2,0,1:T(8,128)}, s32[]{:T(128)}, s32[64]{0:T(128)S(1)}, /*index=5*/s32[]{:T(128)}...) while((s32[]{:T(128)}, f32[32,2048,128]{2,0,1:T(8,128)}, ...), condition=%wide.region_3.6_spmd.clone, body=%wide.region_0.5_spmd.clone.sunk | while | flops 1049155 | bytes 10487937 | solution.py:85
  236.9 2.7 broadcast_multiply_fusion.8
  239.6 9.0 scatter_fusion
  248.6 8.0 scatter_fusion.1
  256.7 4.5 copy_bitcast_fusion.5
  261.2 22.8 %copy_bitcast_fusion.1 = f32[32,262144]{1,0:T(8,128)} fusion(f32[32,2048,128]{2,0,1:T(8,128)} %get-tuple-element.609), kind=kLoop, calls=%fused_computation.69 | loop fusion | bytes 67108864 | tf_op jit(solution)/shard_map/reshape | solution.py:102
  284.1 39.0 %reduce-scatter.7.cloned.1.call-done = f32[32,16384]{1,0:T(8,128)} async-done(((f32[32,32768]{1,0:T(8,128)}), f32[32,16384]{1,0:T(8,128)}) %reduce-scatter.7.cloned.1.call-update) | async-done | bytes 2097168 | tf_op jit(solution)/shard_map/reduce_scatter | solution.py:104
  323.0 337.6 %reduce-scatter.5.cloned.1.call-done = f32[32,16384]{1,0:T(8,128)} async-done(((f32[32,262144]{1,0:T(8,128)}), f32[32,16384]{1,0:T(8,128)}) %reduce-scatter.5.cloned.1.call-update) | async-done | bytes 2097168 | tf_op jit(solution)/shard_map/reduce_scatter | solution.py:101
  660.6 2.4 add.419
  666.1 39.2 %psum.14 = f32[32,32]{1,0:T(8,128)S(1)} all-reduce(f32[32,32]{1,0:T(8,128)S(1)} %fusion.52), channel_id=1, replica_groups=mesh['row'=2,'col'=16] {'row','col'}, use_global_device_ids=true, to_apply=%region_6.9 | all-reduce | flops 1024 | bytes 8192 | tf_op jit(solution)/shard_map/psum | solution.py:111
  705.4 57.9 %while.92 = (s32[]{:T(128)}, f32[32,32]{1,0:T(8,128)S(1)}, f32[32,32]{0,1:T(8,128)S(1)}, s32[]{:T(128)}, s32[]{:T(128)}) while((s32[]{:T(128)}, f32[32,32]{1,0:T(8,128)S(1)}, f32[32,32]{0,1:T(8,128)S(1)}, s32[]{:T(128)}, s32[]{:T(128)}) %tuple.195), condition=%wide.region_10.13_spmd.clone.clone, body=%wide.region_7.12_spmd.clone.clone.sunk | while | flops 2401 | bytes 8913 | solution.py:42
  763.4 48.8 %while.93 = (s32[]{:T(128)}, f32[32,32]{1,0:T(8,128)S(1)}, f32[32,32]{1,0:T(8,128)S(1)}, s32[]{:T(128)}, s32[]{:T(128)}) while((s32[]{:T(128)}, f32[32,32]{1,0:T(8,128)S(1)}, f32[32,32]{1,0:T(8,128)S(1)}, s32[]{:T(128)}, s32[]{:T(128)}) %tuple.198), condition=%wide.region_14.17_spmd.clone.clone, body=%wide.region_11.16_spmd.clone.clone.sunk | while | flops 2305 | bytes 6221 | solution.py:59
  812.2 5.9 broadcast.334
  818.1 2.9 constant_dynamic-update-slice_fusion.15
  820.9 4.4 collective-permute-start.16
  825.5 12.6 collective-permute-done.15
  838.1 8.2 collective-permute-start.17
  850.9 4.6 collective-permute-done.17
  855.4 16.8 %collective-permute-start.19 = (bf16[32,16384]{1,0:T(8,128)(2,1)}, bf16[32,16384]{1,0:T(8,128)(2,1)}, u32[]{:S(2)}, u32[]{:S(2)}) collective-permute-start(bf16[32,16384]{1,0:T(8,128)(2,1)} %collective-permute-done.17), channel_id=1, source_target_pairs={{0,1},{1,2},{2,3},{3,4},{4,5},{5,6},{6,7},{7,8},{8,9},{9,10},{10,1... | collective-permute-start | bytes 3145736 | tf_op jit(solution)/shard_map/ppermute | solution.py:17
  876.7 3.3 copy_bitcast_fusion.6
  884.5 13.5 collective-permute-start.21
  902.5 6.1 collective-permute-done.21
  908.5 15.2 collective-permute-start.23
  926.4 22.7 %collective-permute-start.25 = (bf16[32,16384]{1,0:T(8,128)(2,1)S(1)}, bf16[32,16384]{1,0:T(8,128)(2,1)S(1)}, u32[]{:S(2)}, u32[]{:S(2)}) collective-permute-start(bf16[32,16384]{1,0:T(8,128)(2,1)S(1)} %collective-permute-done.23), channel_id=1, source_target_pairs={{0,1},{1,2},{2,3},{3,4},{4,5},{5,6},{6,7},{7,8},{8,9},{9,10},{10,1... | collective-permute-start | bytes 3145736 | tf_op jit(solution)/shard_map/ppermute | solution.py:17
  951.4 23.1 %collective-permute-start.27 = (bf16[32,16384]{1,0:T(8,128)(2,1)S(1)}, bf16[32,16384]{1,0:T(8,128)(2,1)S(1)}, u32[]{:S(2)}, u32[]{:S(2)}) collective-permute-start(bf16[32,16384]{1,0:T(8,128)(2,1)S(1)} %collective-permute-done.25), channel_id=1, source_target_pairs={{0,1},{1,2},{2,3},{3,4},{4,5},{5,6},{6,7},{7,8},{8,9},{9,10},{10,1... | collective-permute-start | bytes 3145736 | tf_op jit(solution)/shard_map/ppermute | solution.py:17
  976.7 22.8 %collective-permute-start.29 = (bf16[32,16384]{1,0:T(8,128)(2,1)S(1)}, bf16[32,16384]{1,0:T(8,128)(2,1)S(1)}, u32[]{:S(2)}, u32[]{:S(2)}) collective-permute-start(bf16[32,16384]{1,0:T(8,128)(2,1)S(1)} %collective-permute-done.27), channel_id=1, source_target_pairs={{0,1},{1,2},{2,3},{3,4},{4,5},{5,6},{6,7},{7,8},{8,9},{9,10},{10,1... | collective-permute-start | bytes 3145736 | tf_op jit(solution)/shard_map/ppermute | solution.py:17
  1002.9 14.5 copy_bitcast_fusion.2
  1017.4 6.4 gather_fusion.3
  1025.5 11.3 broadcast.332
  1036.8 2.6 broadcast.333
  1039.4 20.4 %while.91 = (s32[]{:T(128)}, f32[32,2048,128]{2,0,1:T(8,128)}, f32[32,256,128]{2,0,1:T(8,128)}, s32[]{:T(128)}, s32[64]{0:T(128)S(1)}, /*index=5*/s32[]{:T(128)}...) while((s32[]{:T(128)}, f32[32,2048,128]{2,0,1:T(8,128)}, ...), condition=%wide.region_18.21_spmd.clone, body=%wide.region_15.20_spmd.clone.sunk | while | flops 1049155 | bytes 10487937 | solution.py:85
  1040.1 2.7 broadcast_multiply_fusion.9
  1042.8 9.0 scatter_fusion.2
  1051.8 8.0 scatter_fusion.3
  1059.8 4.5 copy_bitcast_fusion.4
  1064.6 22.8 %copy_bitcast_fusion = f32[32,262144]{1,0:T(8,128)} fusion(f32[32,2048,128]{2,0,1:T(8,128)} %get-tuple-element.613), kind=kLoop, calls=%fused_computation.68 | loop fusion | bytes 67108864 | tf_op jit(solution)/shard_map/reshape | solution.py:102
  1087.4 43.6 %reduce-scatter.11.cloned.1.call-done = f32[32,16384]{1,0:T(8,128)} async-done(((f32[32,32768]{1,0:T(8,128)}), f32[32,16384]{1,0:T(8,128)}) %reduce-scatter.11.cloned.1.call-update) | async-done | bytes 2097168 | tf_op jit(solution)/shard_map/reduce_scatter | solution.py:104
  1131.0 336.8 %reduce-scatter.9.cloned.1.call-done = f32[32,16384]{1,0:T(8,128)} async-done(((f32[32,262144]{1,0:T(8,128)}), f32[32,16384]{1,0:T(8,128)}) %reduce-scatter.9.cloned.1.call-update) | async-done | bytes 2097168 | tf_op jit(solution)/shard_map/reduce_scatter | solution.py:101
  1467.9 2.4 add.420
  1473.4 39.0 %psum.15 = f32[32,32]{1,0:T(8,128)S(1)} all-reduce(f32[32,32]{1,0:T(8,128)S(1)} %fusion.53), channel_id=1, replica_groups=mesh['row'=2,'col'=16] {'row','col'}, use_global_device_ids=true, to_apply=%region_21.24 | all-reduce | flops 1024 | bytes 8192 | tf_op jit(solution)/shard_map/psum | solution.py:111
  1512.5 57.4 %while.94 = (s32[]{:T(128)}, f32[32,32]{1,0:T(8,128)S(1)}, f32[32,32]{0,1:T(8,128)S(1)}, s32[]{:T(128)}, s32[]{:T(128)}) while((s32[]{:T(128)}, f32[32,32]{1,0:T(8,128)S(1)}, f32[32,32]{0,1:T(8,128)S(1)}, s32[]{:T(128)}, s32[]{:T(128)}) %tuple.204), condition=%wide.region_25.28_spmd.clone.clone, body=%wide.region_22.27_spmd.clone.clone.sunk | while | flops 2401 | bytes 8913 | solution.py:42
  1569.9 42.1 %while.95 = (s32[]{:T(128)}, f32[32,32]{1,0:T(8,128)S(1)}, f32[32,32]{1,0:T(8,128)S(1)}, s32[]{:T(128)}, s32[]{:T(128)}) while((s32[]{:T(128)}, f32[32,32]{1,0:T(8,128)S(1)}, f32[32,32]{1,0:T(8,128)S(1)}, s32[]{:T(128)}, s32[]{:T(128)}) %tuple.207), condition=%wide.region_29.32_spmd.clone.clone, body=%wide.region_26.31_spmd.clone.clone.sunk | while | flops 2305 | bytes 6221 | solution.py:59
  1612.0 4.8 fusion.54
  (762 shorter events, 226.8 us)
Async XLA Ops:
  6.5 68.9 %copy-start = (bf16[64,128,128]{2,1,0:T(8,128)(2,1)S(1)}, bf16[64,128,128]{2,1,0:T(8,128)(2,1)}, u32[]{:S(2)}) copy-start(bf16[64,128,128]{2,1,0:T(8,128)(2,1)} %param.21) | copy-start | bytes 6291460
  6.5 14.3 copy-start.7
  6.5 14.3 copy-start.8
  6.5 63.4 %all-gather.3.cloned.1.call-start = ((), (), s32[]{:S(2)}) async-start(), calls=%async_computation.4 | async-start | bytes 3145728 | tf_op jit(solution)/shard_map/all_gather | solution.py:96
  6.6 6.7 copy-start.6
  14.3 5.4 copy-start.4
  14.3 18.1 %collective-permute-start = (bf16[32,16384]{1,0:T(8,128)(2,1)S(1)}, bf16[32,16384]{1,0:T(8,128)(2,1)}, u32[]{:S(2)}, u32[]{:S(2)}) collective-permute-start(bf16[32,16384]{1,0:T(8,128)(2,1)S(1)} %get-tuple-element.808), channel_id=1, source_target_pairs={{0,1},{1,2},{2,3},{3,4},{4,5},{5,6},{6,7},{7,8},{8,9},{9,10},{10,1... | collective-permute-start | bytes 3145736 | tf_op jit(solution)/shard_map/ppermute | solution.py:17
  14.8 25.6 %collective-permute-start.1 = (bf16[32,16384]{1,0:T(8,128)(2,1)S(1)}, bf16[32,16384]{1,0:T(8,128)(2,1)}, u32[]{:S(2)}, u32[]{:S(2)}) collective-permute-start(bf16[32,16384]{1,0:T(8,128)(2,1)S(1)} %get-tuple-element.808), channel_id=1, source_target_pairs={{0,15},{1,0},{2,1},{3,2},{4,3},{5,4},{6,5},{7,6},{8,7},{9,8},{10,9... | collective-permute-start | bytes 3145736 | tf_op jit(solution)/shard_map/ppermute | solution.py:20
  19.8 303.2 %reduce-scatter.7.cloned.1.call-start = ((), (), s32[]{:S(2)}) async-start(), calls=%async_computation.6 | async-start | bytes 6291456 | tf_op jit(solution)/shard_map/reduce_scatter | solution.py:104
  32.5 17.3 %collective-permute-start.2 = (bf16[32,16384]{1,0:T(8,128)(2,1)}, bf16[32,16384]{1,0:T(8,128)(2,1)}, u32[]{:S(2)}, u32[]{:S(2)}) collective-permute-start(bf16[32,16384]{1,0:T(8,128)(2,1)} %collective-permute-done), channel_id=1, source_target_pairs={{0,1},{1,2},{2,3},{3,4},{4,5},{5,6},{6,7},{7,8},{8,9},{9,10},{10,1... | collective-permute-start | bytes 3145736 | tf_op jit(solution)/shard_map/ppermute | solution.py:17
  40.4 25.0 %collective-permute-start.3 = (bf16[32,16384]{1,0:T(8,128)(2,1)}, bf16[32,16384]{1,0:T(8,128)(2,1)}, u32[]{:S(2)}, u32[]{:S(2)}) collective-permute-start(bf16[32,16384]{1,0:T(8,128)(2,1)} %collective-permute-done.1), channel_id=1, source_target_pairs={{0,15},{1,0},{2,1},{3,2},{4,3},{5,4},{6,5},{7,6},{8,7},{9,8},{10,9... | collective-permute-start | bytes 3145736 | tf_op jit(solution)/shard_map/ppermute | solution.py:20
  49.8 27.8 %collective-permute-start.4 = (bf16[32,16384]{1,0:T(8,128)(2,1)}, bf16[32,16384]{1,0:T(8,128)(2,1)}, u32[]{:S(2)}, u32[]{:S(2)}) collective-permute-start(bf16[32,16384]{1,0:T(8,128)(2,1)} %collective-permute-done.2), channel_id=1, source_target_pairs={{0,1},{1,2},{2,3},{3,4},{4,5},{5,6},{6,7},{7,8},{8,9},{9,10},{10,1... | collective-permute-start | bytes 3145736 | tf_op jit(solution)/shard_map/ppermute | solution.py:17
  65.4 26.9 %collective-permute-start.5 = (bf16[32,16384]{1,0:T(8,128)(2,1)}, bf16[32,16384]{1,0:T(8,128)(2,1)}, u32[]{:S(2)}, u32[]{:S(2)}) collective-permute-start(bf16[32,16384]{1,0:T(8,128)(2,1)} %collective-permute-done.3), channel_id=1, source_target_pairs={{0,15},{1,0},{2,1},{3,2},{4,3},{5,4},{6,5},{7,6},{8,7},{9,8},{10,9... | collective-permute-start | bytes 3145736 | tf_op jit(solution)/shard_map/ppermute | solution.py:20
  77.6 29.3 %collective-permute-start.6 = (bf16[32,16384]{1,0:T(8,128)(2,1)}, bf16[32,16384]{1,0:T(8,128)(2,1)S(1)}, u32[]{:S(2)}, u32[]{:S(2)}) collective-permute-start(bf16[32,16384]{1,0:T(8,128)(2,1)} %collective-permute-done.4), channel_id=1, source_target_pairs={{0,1},{1,2},{2,3},{3,4},{4,5},{5,6},{6,7},{7,8},{8,9},{9,10},{10,1... | collective-permute-start | bytes 3145736 | tf_op jit(solution)/shard_map/ppermute | solution.py:17
  92.2 24.8 %collective-permute-start.7 = (bf16[32,16384]{1,0:T(8,128)(2,1)}, bf16[32,16384]{1,0:T(8,128)(2,1)S(1)}, u32[]{:S(2)}, u32[]{:S(2)}) collective-permute-start(bf16[32,16384]{1,0:T(8,128)(2,1)} %collective-permute-done.5), channel_id=1, source_target_pairs={{0,15},{1,0},{2,1},{3,2},{4,3},{5,4},{6,5},{7,6},{8,7},{9,8},{10,9... | collective-permute-start | bytes 3145736 | tf_op jit(solution)/shard_map/ppermute | solution.py:20
  107.0 17.8 %collective-permute-start.8 = (bf16[32,16384]{1,0:T(8,128)(2,1)S(1)}, bf16[32,16384]{1,0:T(8,128)(2,1)S(1)}, u32[]{:S(2)}, u32[]{:S(2)}) collective-permute-start(bf16[32,16384]{1,0:T(8,128)(2,1)S(1)} %collective-permute-done.6), channel_id=1, source_target_pairs={{0,1},{1,2},{2,3},{3,4},{4,5},{5,6},{6,7},{7,8},{8,9},{9,10},{10,1... | collective-permute-start | bytes 3145736 | tf_op jit(solution)/shard_map/ppermute | solution.py:17
  117.0 24.0 %collective-permute-start.9 = (bf16[32,16384]{1,0:T(8,128)(2,1)S(1)}, bf16[32,16384]{1,0:T(8,128)(2,1)S(1)}, u32[]{:S(2)}, u32[]{:S(2)}) collective-permute-start(bf16[32,16384]{1,0:T(8,128)(2,1)S(1)} %collective-permute-done.7), channel_id=1, source_target_pairs={{0,15},{1,0},{2,1},{3,2},{4,3},{5,4},{6,5},{7,6},{8,7},{9,8},{10,9... | collective-permute-start | bytes 3145736 | tf_op jit(solution)/shard_map/ppermute | solution.py:20
  124.8 23.3 %collective-permute-start.10 = (bf16[32,16384]{1,0:T(8,128)(2,1)S(1)}, bf16[32,16384]{1,0:T(8,128)(2,1)S(1)}, u32[]{:S(2)}, u32[]{:S(2)}) collective-permute-start(bf16[32,16384]{1,0:T(8,128)(2,1)S(1)} %collective-permute-done.8), channel_id=1, source_target_pairs={{0,1},{1,2},{2,3},{3,4},{4,5},{5,6},{6,7},{7,8},{8,9},{9,10},{10,1... | collective-permute-start | bytes 3145736 | tf_op jit(solution)/shard_map/ppermute | solution.py:17
  141.0 24.7 %collective-permute-start.11 = (bf16[32,16384]{1,0:T(8,128)(2,1)S(1)}, bf16[32,16384]{1,0:T(8,128)(2,1)S(1)}, u32[]{:S(2)}, u32[]{:S(2)}) collective-permute-start(bf16[32,16384]{1,0:T(8,128)(2,1)S(1)} %collective-permute-done.9), channel_id=1, source_target_pairs={{0,15},{1,0},{2,1},{3,2},{4,3},{5,4},{6,5},{7,6},{8,7},{9,8},{10,9... | collective-permute-start | bytes 3145736 | tf_op jit(solution)/shard_map/ppermute | solution.py:20
  148.1 25.4 %collective-permute-start.12 = (bf16[32,16384]{1,0:T(8,128)(2,1)S(1)}, bf16[32,16384]{1,0:T(8,128)(2,1)S(1)}, u32[]{:S(2)}, u32[]{:S(2)}) collective-permute-start(bf16[32,16384]{1,0:T(8,128)(2,1)S(1)} %collective-permute-done.10), channel_id=1, source_target_pairs={{0,1},{1,2},{2,3},{3,4},{4,5},{5,6},{6,7},{7,8},{8,9},{9,10},{10,1... | collective-permute-start | bytes 3145736 | tf_op jit(solution)/shard_map/ppermute | solution.py:17
  165.7 25.7 %collective-permute-start.13 = (bf16[32,16384]{1,0:T(8,128)(2,1)S(1)}, bf16[32,16384]{1,0:T(8,128)(2,1)S(1)}, u32[]{:S(2)}, u32[]{:S(2)}) collective-permute-start(bf16[32,16384]{1,0:T(8,128)(2,1)S(1)} %collective-permute-done.11), channel_id=1, source_target_pairs={{0,15},{1,0},{2,1},{3,2},{4,3},{5,4},{6,5},{7,6},{8,7},{9,8},{10,9... | collective-permute-start | bytes 3145736 | tf_op jit(solution)/shard_map/ppermute | solution.py:20
  173.5 25.3 %collective-permute-start.14 = (bf16[32,16384]{1,0:T(8,128)(2,1)S(1)}, bf16[32,16384]{1,0:T(8,128)(2,1)S(1)}, u32[]{:S(2)}, u32[]{:S(2)}) collective-permute-start(bf16[32,16384]{1,0:T(8,128)(2,1)S(1)} %collective-permute-done.12), channel_id=1, source_target_pairs={{0,1},{1,2},{2,3},{3,4},{4,5},{5,6},{6,7},{7,8},{8,9},{9,10},{10,1... | collective-permute-start | bytes 3145736 | tf_op jit(solution)/shard_map/ppermute | solution.py:17
  261.2 399.4 %reduce-scatter.5.cloned.1.call-start = ((), (), s32[]{:S(2)}) async-start(), calls=%async_computation.5 | async-start | bytes 35651584 | tf_op jit(solution)/shard_map/reduce_scatter | solution.py:101
  284.0 592.7 %all-gather.5.cloned.1.call-start = ((), (), s32[]{:S(2)}) async-start(), calls=%async_computation.7 | async-start | bytes 3145728 | tf_op jit(solution)/shard_map/all_gather | solution.py:96
  663.0 1.3 copy-start.1
  812.2 5.9 copy-start.2
  820.9 4.4 copy-start.5
  820.9 17.1 %collective-permute-start.15 = (bf16[32,16384]{1,0:T(8,128)(2,1)S(1)}, bf16[32,16384]{1,0:T(8,128)(2,1)}, u32[]{:S(2)}, u32[]{:S(2)}) collective-permute-start(bf16[32,16384]{1,0:T(8,128)(2,1)S(1)} %get-tuple-element.822), channel_id=1, source_target_pairs={{0,1},{1,2},{2,3},{3,4},{4,5},{5,6},{6,7},{7,8},{8,9},{9,10},{10,1... | collective-permute-start | bytes 3145736 | tf_op jit(solution)/shard_map/ppermute | solution.py:17
  820.9 27.6 %collective-permute-start.16 = (bf16[32,16384]{1,0:T(8,128)(2,1)S(1)}, bf16[32,16384]{1,0:T(8,128)(2,1)}, u32[]{:S(2)}, u32[]{:S(2)}) collective-permute-start(bf16[32,16384]{1,0:T(8,128)(2,1)S(1)} %get-tuple-element.822), channel_id=1, source_target_pairs={{0,15},{1,0},{2,1},{3,2},{4,3},{5,4},{6,5},{7,6},{8,7},{9,8},{10,9... | collective-permute-start | bytes 3145736 | tf_op jit(solution)/shard_map/ppermute | solution.py:20
  825.4 305.6 %reduce-scatter.11.cloned.1.call-start = ((), (), s32[]{:S(2)}) async-start(), calls=%async_computation.9 | async-start | bytes 6291456 | tf_op jit(solution)/shard_map/reduce_scatter | solution.py:104
  838.1 17.3 %collective-permute-start.17 = (bf16[32,16384]{1,0:T(8,128)(2,1)}, bf16[32,16384]{1,0:T(8,128)(2,1)}, u32[]{:S(2)}, u32[]{:S(2)}) collective-permute-start(bf16[32,16384]{1,0:T(8,128)(2,1)} %collective-permute-done.15), channel_id=1, source_target_pairs={{0,1},{1,2},{2,3},{3,4},{4,5},{5,6},{6,7},{7,8},{8,9},{9,10},{10,1... | collective-permute-start | bytes 3145736 | tf_op jit(solution)/shard_map/ppermute | solution.py:17
  848.6 25.9 %collective-permute-start.18 = (bf16[32,16384]{1,0:T(8,128)(2,1)}, bf16[32,16384]{1,0:T(8,128)(2,1)}, u32[]{:S(2)}, u32[]{:S(2)}) collective-permute-start(bf16[32,16384]{1,0:T(8,128)(2,1)} %collective-permute-done.16), channel_id=1, source_target_pairs={{0,15},{1,0},{2,1},{3,2},{4,3},{5,4},{6,5},{7,6},{8,7},{9,8},{10,9... | collective-permute-start | bytes 3145736 | tf_op jit(solution)/shard_map/ppermute | solution.py:20
  855.4 29.1 %collective-permute-start.19 = (bf16[32,16384]{1,0:T(8,128)(2,1)}, bf16[32,16384]{1,0:T(8,128)(2,1)}, u32[]{:S(2)}, u32[]{:S(2)}) collective-permute-start(bf16[32,16384]{1,0:T(8,128)(2,1)} %collective-permute-done.17), channel_id=1, source_target_pairs={{0,1},{1,2},{2,3},{3,4},{4,5},{5,6},{6,7},{7,8},{8,9},{9,10},{10,1... | collective-permute-start | bytes 3145736 | tf_op jit(solution)/shard_map/ppermute | solution.py:17
  874.5 25.8 %collective-permute-start.20 = (bf16[32,16384]{1,0:T(8,128)(2,1)}, bf16[32,16384]{1,0:T(8,128)(2,1)}, u32[]{:S(2)}, u32[]{:S(2)}) collective-permute-start(bf16[32,16384]{1,0:T(8,128)(2,1)} %collective-permute-done.18), channel_id=1, source_target_pairs={{0,15},{1,0},{2,1},{3,2},{4,3},{5,4},{6,5},{7,6},{8,7},{9,8},{10,9... | collective-permute-start | bytes 3145736 | tf_op jit(solution)/shard_map/ppermute | solution.py:20
  884.5 24.1 %collective-permute-start.21 = (bf16[32,16384]{1,0:T(8,128)(2,1)}, bf16[32,16384]{1,0:T(8,128)(2,1)S(1)}, u32[]{:S(2)}, u32[]{:S(2)}) collective-permute-start(bf16[32,16384]{1,0:T(8,128)(2,1)} %collective-permute-done.19), channel_id=1, source_target_pairs={{0,1},{1,2},{2,3},{3,4},{4,5},{5,6},{6,7},{7,8},{8,9},{9,10},{10,1... | collective-permute-start | bytes 3145736 | tf_op jit(solution)/shard_map/ppermute | solution.py:17
  900.2 24.5 %collective-permute-start.22 = (bf16[32,16384]{1,0:T(8,128)(2,1)}, bf16[32,16384]{1,0:T(8,128)(2,1)S(1)}, u32[]{:S(2)}, u32[]{:S(2)}) collective-permute-start(bf16[32,16384]{1,0:T(8,128)(2,1)} %collective-permute-done.20), channel_id=1, source_target_pairs={{0,15},{1,0},{2,1},{3,2},{4,3},{5,4},{6,5},{7,6},{8,7},{9,8},{10,9... | collective-permute-start | bytes 3145736 | tf_op jit(solution)/shard_map/ppermute | solution.py:20
  908.5 17.8 %collective-permute-start.23 = (bf16[32,16384]{1,0:T(8,128)(2,1)S(1)}, bf16[32,16384]{1,0:T(8,128)(2,1)S(1)}, u32[]{:S(2)}, u32[]{:S(2)}) collective-permute-start(bf16[32,16384]{1,0:T(8,128)(2,1)S(1)} %collective-permute-done.21), channel_id=1, source_target_pairs={{0,1},{1,2},{2,3},{3,4},{4,5},{5,6},{6,7},{7,8},{8,9},{9,10},{10,1... | collective-permute-start | bytes 3145736 | tf_op jit(solution)/shard_map/ppermute | solution.py:17
  924.7 25.4 %collective-permute-start.24 = (bf16[32,16384]{1,0:T(8,128)(2,1)S(1)}, bf16[32,16384]{1,0:T(8,128)(2,1)S(1)}, u32[]{:S(2)}, u32[]{:S(2)}) collective-permute-start(bf16[32,16384]{1,0:T(8,128)(2,1)S(1)} %collective-permute-done.22), channel_id=1, source_target_pairs={{0,15},{1,0},{2,1},{3,2},{4,3},{5,4},{6,5},{7,6},{8,7},{9,8},{10,9... | collective-permute-start | bytes 3145736 | tf_op jit(solution)/shard_map/ppermute | solution.py:20
  926.4 25.0 %collective-permute-start.25 = (bf16[32,16384]{1,0:T(8,128)(2,1)S(1)}, bf16[32,16384]{1,0:T(8,128)(2,1)S(1)}, u32[]{:S(2)}, u32[]{:S(2)}) collective-permute-start(bf16[32,16384]{1,0:T(8,128)(2,1)S(1)} %collective-permute-done.23), channel_id=1, source_target_pairs={{0,1},{1,2},{2,3},{3,4},{4,5},{5,6},{6,7},{7,8},{8,9},{9,10},{10,1... | collective-permute-start | bytes 3145736 | tf_op jit(solution)/shard_map/ppermute | solution.py:17
  950.1 25.4 %collective-permute-start.26 = (bf16[32,16384]{1,0:T(8,128)(2,1)S(1)}, bf16[32,16384]{1,0:T(8,128)(2,1)S(1)}, u32[]{:S(2)}, u32[]{:S(2)}) collective-permute-start(bf16[32,16384]{1,0:T(8,128)(2,1)S(1)} %collective-permute-done.24), channel_id=1, source_target_pairs={{0,15},{1,0},{2,1},{3,2},{4,3},{5,4},{6,5},{7,6},{8,7},{9,8},{10,9... | collective-permute-start | bytes 3145736 | tf_op jit(solution)/shard_map/ppermute | solution.py:20
  951.4 25.4 %collective-permute-start.27 = (bf16[32,16384]{1,0:T(8,128)(2,1)S(1)}, bf16[32,16384]{1,0:T(8,128)(2,1)S(1)}, u32[]{:S(2)}, u32[]{:S(2)}) collective-permute-start(bf16[32,16384]{1,0:T(8,128)(2,1)S(1)} %collective-permute-done.25), channel_id=1, source_target_pairs={{0,1},{1,2},{2,3},{3,4},{4,5},{5,6},{6,7},{7,8},{8,9},{9,10},{10,1... | collective-permute-start | bytes 3145736 | tf_op jit(solution)/shard_map/ppermute | solution.py:17
  975.5 25.1 %collective-permute-start.28 = (bf16[32,16384]{1,0:T(8,128)(2,1)S(1)}, bf16[32,16384]{1,0:T(8,128)(2,1)S(1)}, u32[]{:S(2)}, u32[]{:S(2)}) collective-permute-start(bf16[32,16384]{1,0:T(8,128)(2,1)S(1)} %collective-permute-done.26), channel_id=1, source_target_pairs={{0,15},{1,0},{2,1},{3,2},{4,3},{5,4},{6,5},{7,6},{8,7},{9,8},{10,9... | collective-permute-start | bytes 3145736 | tf_op jit(solution)/shard_map/ppermute | solution.py:20
  976.7 25.1 %collective-permute-start.29 = (bf16[32,16384]{1,0:T(8,128)(2,1)S(1)}, bf16[32,16384]{1,0:T(8,128)(2,1)S(1)}, u32[]{:S(2)}, u32[]{:S(2)}) collective-permute-start(bf16[32,16384]{1,0:T(8,128)(2,1)S(1)} %collective-permute-done.27), channel_id=1, source_target_pairs={{0,1},{1,2},{2,3},{3,4},{4,5},{5,6},{6,7},{7,8},{8,9},{9,10},{10,1... | collective-permute-start | bytes 3145736 | tf_op jit(solution)/shard_map/ppermute | solution.py:17
  1064.3 403.6 %reduce-scatter.9.cloned.1.call-start = ((), (), s32[]{:S(2)}) async-start(), calls=%async_computation.8 | async-start | bytes 35651584 | tf_op jit(solution)/shard_map/reduce_scatter | solution.py:101
  1470.3 1.3 copy-start.3
Sparse Core Ops, SparseCore 0:
  19.9 32.1 all-gather.2
  261.3 61.7 reduce-scatter.6
  327.9 332.6 reduce-scatter.4
  825.5 31.1 all-gather.4
  1064.4 66.5 reduce-scatter.10
  1135.1 332.6 reduce-scatter.8
